TPU v7x, 32 devices: a whole 2x2x4 slice. The times are simulated.
32 devices in a mesh: tenant: 2 (over x), store: 16 (over z, y, core).
Axes of the slice: x: 2, y: 2, z: 4, core: 2. Of those that a mesh axis runs over, the one named last changes fastest.
Arguments:
- queries: bfloat16 [4096, 1024], P(('tenant', 'store')), parts along dimension 0, may hold values from -24 to 24
- own_kv: bfloat16 [4096, 256], P(('tenant', 'store')), parts along dimension 0, may hold values from -15 to 15
- store_kv: bfloat16 [1024, 256, 256], P(('tenant', 'store')), parts along dimension 0, may hold values from -15 to 15
- q_start: int32 [32], P(('tenant', 'store')), parts along dimension 0, may hold values from 12288 to 16255
- pop_ids: int32 [8], P('tenant'), parts along dimension 0, may hold values from 0 to 511
- pop_pos: int32 [32, 4], P(('tenant', 'store')), parts along dimension 0, may hold values from 0 to 12287
- rare_ids: int32 [32, 6], P(('tenant', 'store')), parts along dimension 0, may hold values from 0 to 511, as said below
- rare_count: int32 [32], P(('tenant', 'store')), parts along dimension 0, may hold values from 4 to 6, as said below
- rare_pos: int32 [32, 6], P(('tenant', 'store')), parts along dimension 0, may hold values from 0 to 12287
Outputs:
- attended: bfloat16 [4096, 1024], P(('tenant', 'store')), parts along dimension 0
There are 2 independent parts, one for each index of `tenant`. A program takes and returns all parts, laid end to end along the dimension named above; each array names one. Nothing has to cross between parts.
Inputs may be any that keep to these rules, and one draw needn't show every extreme that they name: `rare_ids`: the first rare_count entries of one device's list name blocks of different holders (id // 32); entries after them are ignored. `rare_count`: some device requests exactly 6 blocks and another exactly 4.
All inputs are finite; a program needn't handle non-finite values.
Results may differ from a plain program's by a relative error of at most 0.0085.
The roundings to bfloat16 on the way count: a program that leaves them out, or rounds other values in their place, can miss the bound.
Values may be sent and summed in bfloat16 or wider, within the bound.
A program may use at most 128 MiB of HBM per device.

v0:
```python
import jax
import jax.numpy as jnp
from jax import lax
from jax.sharding import PartitionSpec as P


def rotate(values, positions, head_size):
    half_size = head_size // 2
    freq_table = 500000.0 ** (-(2.0 * jnp.arange(half_size, dtype=jnp.float32)) / head_size)
    angles = positions.astype(jnp.float32)[:, None] * freq_table[None, :]
    cosine = jnp.cos(angles)[:, None, :]
    sine_part = jnp.sin(angles)[:, None, :]
    shaped = values.reshape(values.shape[0], -1, 2, half_size)
    first_half = shaped[:, :, 0, :]
    second_half = shaped[:, :, 1, :]
    turned = jnp.stack(
        [
            first_half * cosine - second_half * sine_part,
            second_half * cosine + first_half * sine_part,
        ],
        axis=2,
    )
    return turned.reshape(values.shape)


def block_stats(query_rows, key_rows, value_rows, allowed, scale_factor):
    scores = jnp.dot(query_rows, key_rows.T, preferred_element_type=jnp.float32) * scale_factor
    scores = jnp.where(allowed, scores, -jnp.inf)
    top_score = jnp.max(scores, axis=1)
    weights = jnp.exp(scores - top_score[:, None]).astype(jnp.bfloat16)
    weight_sum = jnp.sum(weights.astype(jnp.float32), axis=1)
    mixed_part = jnp.dot(weights, value_rows, preferred_element_type=jnp.float32)
    return (top_score, weight_sum, mixed_part)


def combine(running, top_score, weight_sum, mixed_part):
    old_top, old_sum, old_mixed = running
    peak = jnp.maximum(old_top, top_score)
    keep_factor = jnp.exp(old_top - peak)
    take_factor = jnp.exp(top_score - peak)
    return (
        peak,
        old_sum * keep_factor + weight_sum * take_factor,
        old_mixed * keep_factor[:, None] + mixed_part * take_factor[:, None],
    )


def span_fold(running, query_rows, span_kv, offset, head_size, scale_factor):
    span_len = span_kv.shape[0]
    span_keys = rotate(
        span_kv[:, :head_size].astype(jnp.float32),
        offset + jnp.arange(span_len, dtype=jnp.int32),
        head_size,
    ).astype(jnp.bfloat16)
    top_score, weight_sum, mixed_part = block_stats(
        query_rows, span_keys, span_kv[:, head_size:], True, scale_factor
    )
    return combine(running, top_score, weight_sum, mixed_part)


def body(queries, own_kv, store_kv, q_start, pop_ids, pop_pos, rare_ids, rare_count, rare_pos):
    own_index = lax.axis_index("store")
    store_count = lax.axis_size("store")
    token_count = queries.shape[0]
    head_size = own_kv.shape[1] // 2
    group_size = queries.shape[1] // head_size
    per_device = store_kv.shape[0]
    span_len = store_kv.shape[1]
    kv_width = store_kv.shape[2]
    request_most = rare_ids.shape[1]
    scale_factor = head_size ** (-0.5)
    positions = q_start[0] + jnp.arange(token_count, dtype=jnp.int32)
    query_rows = (
        rotate(queries.astype(jnp.float32), positions, head_size)
        .astype(jnp.bfloat16)
        .reshape(token_count * group_size, head_size)
    )
    own_keys = rotate(own_kv[:, :head_size].astype(jnp.float32), positions, head_size).astype(
        jnp.bfloat16
    )
    causal = (jnp.arange(token_count * group_size) // group_size)[:, None] >= jnp.arange(
        token_count
    )[None, :]
    running = block_stats(query_rows, own_keys, own_kv[:, head_size:], causal, scale_factor)
    rare_list = rare_ids[0]
    is_request = jnp.arange(request_most) < rare_count[0]
    holder_index = rare_list // per_device
    slot_index = rare_list % per_device
    match_table = (
        holder_index[:, None] == jnp.arange(store_count, dtype=jnp.int32)[None, :]
    ) & is_request[:, None]
    asked = jnp.sum(jnp.where(match_table, slot_index[:, None] + 1, 0), axis=0) - 1
    asked_pos = jnp.sum(jnp.where(match_table, rare_pos[0][:, None], 0), axis=0)
    packed = jnp.stack([asked, asked_pos], axis=1)
    incoming = lax.all_to_all(packed, "store", split_axis=0, concat_axis=0, tiled=True)
    wanted_slot = incoming[:, 0]
    reply = jnp.take(store_kv, jnp.clip(wanted_slot, 0, per_device - 1), axis=0)
    reply = jnp.where((wanted_slot >= 0)[:, None, None], reply, jnp.zeros_like(reply))
    received = lax.all_to_all(reply, "store", split_axis=0, concat_axis=0, tiled=True)
    picked = jnp.take(store_kv, pop_ids % per_device, axis=0)
    holds_it = (pop_ids // per_device == own_index)[:, None, None]
    summed = lax.psum(jnp.where(holds_it, picked.astype(jnp.float32), 0.0), "store")
    popular_kv = summed.astype(jnp.bfloat16)
    for pop_index in range(pop_ids.shape[0]):
        running = span_fold(
            running,
            query_rows,
            popular_kv[pop_index],
            pop_pos[0, pop_index],
            head_size,
            scale_factor,
        )
    rare_kv = jnp.take(received, holder_index, axis=0)
    pair_count = request_most // 2
    paired_kv = rare_kv.reshape(pair_count, 2, span_len, kv_width)
    paired_pos = rare_pos[0].reshape(pair_count, 2)
    paired_live = is_request.reshape(pair_count, 2)

    def rare_step(carry, inputs):
        pair_kv, pair_pos, pair_live = inputs
        key_pos = (pair_pos[:, None] + jnp.arange(span_len, dtype=jnp.int32)[None, :]).reshape(-1)
        flat_kv = pair_kv.reshape(2 * span_len, kv_width)
        pair_keys = (
            rotate(flat_kv[:, :head_size].astype(jnp.float32), key_pos, head_size)
            .astype(jnp.bfloat16)
            .reshape(2, span_len, head_size)
        )
        scores = (
            jnp.einsum("rd,ckd->crk", query_rows, pair_keys, preferred_element_type=jnp.float32)
            * scale_factor
        )
        top_score = jnp.max(scores, axis=2)
        weights = jnp.exp(scores - top_score[:, :, None]).astype(jnp.bfloat16)
        weight_sum = jnp.sum(weights.astype(jnp.float32), axis=2)
        mixed_part = jnp.einsum(
            "crk,ckd->crd", weights, pair_kv[:, :, head_size:], preferred_element_type=jnp.float32
        )
        top_score = jnp.where(pair_live[:, None], top_score, -jnp.inf)
        carry = combine(carry, top_score[0], weight_sum[0], mixed_part[0])
        carry = combine(carry, top_score[1], weight_sum[1], mixed_part[1])
        return (carry, None)

    running, unused_out = lax.scan(rare_step, running, (paired_kv, paired_pos, paired_live))
    final_top, final_sum, final_mixed = running
    attended = final_mixed / final_sum[:, None]
    return attended.reshape(token_count, group_size * head_size).astype(jnp.bfloat16)


def solution(mesh):
    in_specs = (
        P(("tenant", "store"), None),
        P(("tenant", "store"), None),
        P(("tenant", "store"), None, None),
        P(("tenant", "store")),
        P("tenant"),
        P(("tenant", "store"), None),
        P(("tenant", "store"), None),
        P(("tenant", "store")),
        P(("tenant", "store"), None),
    )
    out_specs = P(("tenant", "store"), None)
    return jax.shard_map(body, mesh=mesh, in_specs=in_specs, out_specs=out_specs, check_vma=False)
```

profile of v0, /device:TPU:13, one launch (start us, length us, event | category | flops | bytes accessed | tf_op | source)
XLA Modules:
  0.0 171.5 jit_solution(15668158300816286855)
XLA Ops:
  0.0 0.7 and_select_fusion.2
  1.3 0.7 select_reduce_fusion.1
  2.1 0.7 copy.49
  2.8 6.6 %all-to-all-start = ((s32[16,1,2]{2,1,0:T(1,128)}), s32[16,1,2]{2,1,0:T(1,128)S(1)}, u32[]{:S(2)}, u32[]{:S(2)}) async-start(s32[16,1,2]{2,1,0:T(1,128)} %copy.49), calls=%async_computation | async-start | bytes 16384 | tf_op jit(solution)/shard_map/all_to_all | solution.py:95
  9.3 0.7 fusion.83
  10.0 0.7 compare_and_fusion.1
  10.7 2.8 %gather_fusion = bf16[4,256,256]{2,1,0:T(8,128)(2,1)S(1)} fusion(bf16[32,256,256]{2,1,0:T(8,128)(2,1)} %param.13, s32[1024]{0:T(1024)S(1)} %pad_clamp_fusion.2), kind=kCustom, calls=%fused_computation | custom fusion | bytes 1048592 | tf_op jit(solution)/shard_map/jit(_take)/gather | solution.py:100
  13.7 55.2 %all-reduce.1 = bf16[4,256,256]{2,1,0:T(8,128)(2,1)S(1)} all-reduce(f32[4,256,256]{2,1,0:T(8,128)S(1)} %convert_select_fusion), channel_id=1, replica_groups=mesh['tenant'=2,'store'=16] {'store'}, use_global_device_ids=true, to_apply=%region_1.2 | all-reduce | flops 262144 | bytes 1572864 | tf_op jit(solution)/shard_map/psum | solution.py:102
  69.3 0.6 fusion.89
  70.0 0.6 add_convert_fusion.3
  71.9 0.5 copy.43
  72.7 0.6 add_convert_fusion.2
  73.8 1.2 add_convert_fusion
  75.0 0.8 fusion.60
  75.8 0.6 pad_maximum_fusion.1
  76.8 0.6 pad_maximum_fusion.4
  77.7 0.5 broadcast.810
  78.2 0.6 reduce.6
  78.8 0.6 reduce.7
  79.5 0.7 reshape_squeeze.3
  80.2 0.6 compare_bitcast_fusion
  80.8 2.9 %gather_fusion.1 = bf16[16,256,256]{2,1,0:T(8,128)(2,1)S(1)} fusion(bf16[32,256,256]{2,1,0:T(8,128)(2,1)} %param.13, s32[1024]{0:T(1024)S(1)} %pad_clamp_fusion.1), kind=kCustom, calls=%fused_computation.1 | custom fusion | bytes 4194368 | tf_op jit(solution)/shard_map/jit(_take)/gather | solution.py:97
  83.7 2.3 %select_select_fusion = bf16[16,256,256]{2,1,0:T(8,128)(2,1)} fusion(bf16[16,256,256]{2,1,0:T(8,128)(2,1)S(1)} %gather_fusion.1, pred[16]{0:T(512)(128)(4,1)} %get-tuple-element.114, pred[16]{0:T(512)(128)(4,1)} %get-tuple-element.113), kind=kLoop, calls=%fused_computation.44 | loop fusion | flops 2097152 | bytes 4194336 | tf_op jit(solution)/shard_map/jit(_where)/select_n | solution.py:98
  85.9 22.9 %all-to-all-start.1 = ((bf16[16,256,256]{2,1,0:T(8,128)(2,1)}), bf16[16,256,256]{2,1,0:T(8,128)(2,1)}, u32[]{:S(2)}, u32[]{:S(2)}) async-start(bf16[16,256,256]{2,1,0:T(8,128)(2,1)} %select_select_fusion), calls=%async_computation.1 | async-start | bytes 4194304 | tf_op jit(solution)/shard_map/all_to_all | solution.py:99
  111.6 0.5 fusion.30
  112.1 0.5 fusion.28
  112.7 0.5 fusion.26
  113.5 42.9 %all-to-all-done.1 = bf16[16,256,256]{2,1,0:T(8,128)(2,1)} async-done(((bf16[16,256,256]{2,1,0:T(8,128)(2,1)}), bf16[16,256,256]{2,1,0:T(8,128)(2,1)}, u32[]{:S(2)}, u32[]{:S(2)}) %all-to-all-start.1) | async-done | bytes 2097184 | tf_op jit(solution)/shard_map/all_to_all | solution.py:99
  156.4 2.2 %gather_fusion.2 = bf16[6,256,256]{2,1,0:T(8,128)(2,1)S(1)} fusion(bf16[16,256,256]{2,1,0:T(8,128)(2,1)} %all-to-all-done.1, s32[1024]{0:T(1024)S(1)} %pad_clamp_fusion), kind=kCustom, calls=%fused_computation.2 | custom fusion | bytes 1572888 | tf_op jit(solution)/shard_map/jit(_take)/gather | solution.py:113
  158.7 11.8 %while.14 = (s32[]{:T(128)}, f32[1024]{0:T(1024)S(1)}, f32[1024]{0:T(1024)S(1)}, f32[1024,128]{1,0:T(8,128)S(1)}, pred[3,2]{1,0:T(4,128)(4,1)S(1)}, /*index=5*/b...) while((s32[]{:T(128)}, f32[1024]{0:T(1024)S(1)}, ...), condition=%wide.region_16.17_spmd, body=%wide.region_13.16_spmd.sunk | while | flops 274902208 | bytes 13001355 | solution.py:143
  158.9 0.7 fusion.117
  159.7 0.6 fusion.118
  160.3 0.5 bitcast_reduce_fusion.2
  160.9 0.6 fusion.122
  161.5 0.4 convert_reduce_fusion.7
  162.0 0.6 fusion.123
  162.9 0.7 fusion.117
  163.6 0.6 fusion.118
  164.3 0.5 bitcast_reduce_fusion.2
  164.8 0.6 fusion.122
  165.4 0.4 convert_reduce_fusion.7
  165.9 0.6 fusion.123
  166.8 0.7 fusion.117
  167.5 0.6 fusion.118
  168.2 0.5 bitcast_reduce_fusion.2
  168.7 0.6 fusion.122
  169.9 0.6 fusion.123
  170.7 0.8 convert_element_type.241
  (114 shorter events, 7.8 us)
Async XLA Ops:
  2.8 77.4 %all-to-all-start = ((s32[16,1,2]{2,1,0:T(1,128)}), s32[16,1,2]{2,1,0:T(1,128)S(1)}, u32[]{:S(2)}, u32[]{:S(2)}) async-start(s32[16,1,2]{2,1,0:T(1,128)} %copy.49), calls=%async_computation | async-start | bytes 16384 | tf_op jit(solution)/shard_map/all_to_all | solution.py:95
  13.7 55.7 %copy-start.4 = (s32[1,4]{1,0:T(1,128)S(1)}, s32[1,4]{1,0:T(1,128)}, u32[]{:S(2)}) copy-start(s32[1,4]{1,0:T(1,128)} %param.16) | copy-start | bytes 52
  13.7 57.6 %copy-start = (bf16[128,1024]{1,0:T(8,128)(2,1)S(1)}, bf16[128,1024]{1,0:T(8,128)(2,1)}, u32[]{:S(2)}) copy-start(bf16[128,1024]{1,0:T(8,128)(2,1)} %param.11) | copy-start | bytes 786436
  71.5 1.9 %slice-start = ((bf16[128,256]{1,0:T(8,128)(2,1)}), bf16[128,128]{1,0:T(8,128)(2,1)S(1)}, s32[]{:S(2)}) async-start(bf16[128,256]{1,0:T(8,128)(2,1)} %param.12), calls=%async_computation.2 | async-start | bytes 65536 | tf_op jit(solution)/shard_map/slice | solution.py:78
  71.9 6.4 %copy-start.6 = (s32[1,6]{1,0:T(1,128)S(1)}, s32[1,6]{1,0:T(1,128)}, u32[]{:S(2)}) copy-start(s32[1,6]{1,0:T(1,128)} %param.17) | copy-start | bytes 76
  71.9 6.9 %copy-start.5 = (s32[1,6]{1,0:T(1,128)S(1)}, s32[1,6]{1,0:T(1,128)}, u32[]{:S(2)}) copy-start(s32[1,6]{1,0:T(1,128)} %param.19) | copy-start | bytes 76
  85.9 23.0 %copy-start.1 = (bf16[256,1,2,64]{0,3,2,1:T(8,128)(2,1)S(1)}, bf16[256,1,2,64]{0,3,2,1:T(8,128)(2,1)}, u32[]{:S(2)}) copy-start(bf16[256,1,2,64]{0,3,2,1:T(8,128)(2,1)} %pad_maximum_fusion.1) | copy-start | bytes 196612
  85.9 70.4 %all-to-all-start.1 = ((bf16[16,256,256]{2,1,0:T(8,128)(2,1)}), bf16[16,256,256]{2,1,0:T(8,128)(2,1)}, u32[]{:S(2)}, u32[]{:S(2)}) async-start(bf16[16,256,256]{2,1,0:T(8,128)(2,1)} %select_select_fusion), calls=%async_computation.1 | async-start | bytes 4194304 | tf_op jit(solution)/shard_map/all_to_all | solution.py:99
  109.3 0.8 copy-start.2
  110.5 0.8 copy-start.3
where the time goes:
time: 172 us
  blocking collectives  55.2 us (32%)
  waiting for transfers between devices  42.9 us (25%)
  starting transfers between devices  29.4 us (17%)
  other arithmetic  19 us (11%)
  local copies, waits for them, and re-layouts  15.8 us (9%)
  matrix products  7.16 us (4%)
  between operations  1.76 us (1%)
    psum x1, blocking collectives, body(): lax.psum(jnp.where(holds_it, picked.astype(jnp.float32), 0.0), 'store')  55.2 us
    all_to_all x1, waiting for transfers between devices, body(): lax.all_to_all(reply, 'store', split_axis=0, concat_axis=0, tiled=True)  42.9 us
    all_to_all x1, starting transfers between devices, body(): lax.all_to_all(reply, 'store', split_axis=0, concat_axis=0, tiled=True)  22.9 us
    all_to_all x1, starting transfers between devices, body(): lax.all_to_all(packed, 'store', split_axis=0, concat_axis=0, tiled=True)  6.55 us
  transfers between devices with their start and end apart: 2, of which 1 were waited for; matrix products, arithmetic and copies ran while one was open for 11% of the time, Pallas kernels for 0%

commit v1 on v0

--- a/solution.py
+++ b/solution.py
@@ -99,7 +99,9 @@
     received = lax.all_to_all(reply, "store", split_axis=0, concat_axis=0, tiled=True)
     picked = jnp.take(store_kv, pop_ids % per_device, axis=0)
     holds_it = (pop_ids // per_device == own_index)[:, None, None]
-    summed = lax.psum(jnp.where(holds_it, picked.astype(jnp.float32), 0.0), "store")
+    summed = jnp.sum(
+        lax.all_gather(jnp.where(holds_it, picked.astype(jnp.float32), 0.0), "store"), axis=0
+    )
     popular_kv = summed.astype(jnp.bfloat16)
     for pop_index in range(pop_ids.shape[0]):
         running = span_fold(

time: 172 us -> 209 us (1.22); the launches traced: 172 us -> 206 us
  waiting for transfers between devices: 42.9 us -> 130 us
  blocking collectives: 55.2 us -> 10.1 us
  starting transfers between devices: 29.4 us -> 6.09 us
  between operations: 1.76 us -> 15.1 us
  other arithmetic: 19 us -> 23.6 us
  local copies, waits for them, and re-layouts: 15.8 us -> 12.6 us
    psum x1 -> x0, blocking collectives: 55.2 us -> none  [body(): lax.psum(jnp.where(holds_it, picked.astype(jnp.float32), 0.0), 'store')]
    all_gather x0 -> x1, waiting for transfers between devices: none -> 54.8 us  [body(): lax.all_gather(jnp.where(holds_it, picked.astype(jnp.float32), 0.0), 'sto...]
    all_to_all x1, waiting for transfers between devices: 42.9 us -> 74.7 us  [body(): lax.all_to_all(reply, 'store', split_axis=0, concat_axis=0, tiled=True)]
    all_to_all x1, starting transfers between devices: 22.9 us -> 6.09 us  [body(): lax.all_to_all(reply, 'store', split_axis=0, concat_axis=0, tiled=True)]
    all_to_all x0 -> x1, blocking collectives: none -> 10.1 us  [body(): lax.all_to_all(packed, 'store', split_axis=0, concat_axis=0, tiled=True)]
    reduce_sum x0 -> x1, other arithmetic: none -> 7 us  [body(): jnp.sum(lax.all_gather(jnp.where(holds_it, picked.astype(jnp.float32), 0....]
    all_to_all x1 -> x0, starting transfers between devices: 6.55 us -> none  [body(): lax.all_to_all(packed, 'store', split_axis=0, concat_axis=0, tiled=True)]
  transfers between devices with their start and end apart: 2 -> 2, of which waited for: 1 -> 2; matrix products, arithmetic and copies ran while one was open for 11% -> 7% of each run, Pallas kernels for 0% -> 0%
where the time goes in v1:
time: 209 us; the launch traced here: 206 us
  waiting for transfers between devices  130 us (62%)
  other arithmetic  23.6 us (11%)
  between operations  15.1 us (7%)
  local copies, waits for them, and re-layouts  12.6 us (6%)
  blocking collectives  10.1 us (5%)
  matrix products  8.15 us (4%)
  starting transfers between devices  6.09 us (3%)
    all_to_all x1, waiting for transfers between devices, body(): lax.all_to_all(reply, 'store', split_axis=0, concat_axis=0, tiled=True)  74.7 us
    all_gather x1, waiting for transfers between devices, body(): lax.all_gather(jnp.where(holds_it, picked.astype(jnp.float32), 0.0), 'sto...  54.8 us
    all_to_all x1, blocking collectives, body(): lax.all_to_all(packed, 'store', split_axis=0, concat_axis=0, tiled=True)  10.1 us
    reduce_sum x1, other arithmetic, body(): jnp.sum(lax.all_gather(jnp.where(holds_it, picked.astype(jnp.float32), 0....  7 us
    all_to_all x1, starting transfers between devices, body(): lax.all_to_all(reply, 'store', split_axis=0, concat_axis=0, tiled=True)  6.09 us
  transfers between devices with their start and end apart: 2, of which 2 were waited for; matrix products, arithmetic and copies ran while one was open for 7% of the time, Pallas kernels for 0%

profile of v1, /device:TPU:13, one launch (start us, length us, event | category | flops | bytes accessed | tf_op | source)
XLA Modules:
  0.0 205.6 jit_solution(9913602095612979880)
XLA Ops:
  6.5 0.7 compare_and_fusion.1
  7.2 2.8 %gather_fusion = bf16[4,256,256]{2,1,0:T(8,128)(2,1)S(1)} fusion(bf16[32,256,256]{2,1,0:T(8,128)(2,1)} %param.13, s32[1024]{0:T(1024)S(1)} %pad_clamp_fusion.2), kind=kCustom, calls=%fused_computation | custom fusion | bytes 1048592 | tf_op jit(solution)/shard_map/jit(_take)/gather | solution.py:100
  10.0 1.2 convert_select_fusion
  12.1 10.1 %all_to_all.17 = s32[16,1,2]{2,1,0:T(1,128)S(1)} all-to-all(s32[16,1,2]{2,1,0:T(1,128)S(1)} %copy.39), channel_id=1, replica_groups=mesh['tenant'=2,'store'=16] {'store'}, dimensions={0} | all-to-all | bytes 256 | tf_op jit(solution)/shard_map/all_to_all | solution.py:95
  22.3 3.2 %gather_fusion.1 = bf16[16,256,256]{2,1,0:T(8,128)(2,1)S(1)} fusion(bf16[32,256,256]{2,1,0:T(8,128)(2,1)} %param.13, s32[1024]{0:T(1024)S(1)} %pad_clamp_fusion.1), kind=kCustom, calls=%fused_computation.1 | custom fusion | bytes 4194368 | tf_op jit(solution)/shard_map/jit(_take)/gather | solution.py:97
  25.5 1.7 select_select_fusion
  27.2 6.1 %all-to-all-start.1 = ((bf16[16,256,256]{2,1,0:T(8,128)(2,1)}), bf16[16,256,256]{2,1,0:T(8,128)(2,1)S(1)}, u32[]{:S(2)}, u32[]{:S(2)}) async-start(bf16[16,256,256]{2,1,0:T(8,128)(2,1)} %select_select_fusion), calls=%async_computation.1 | async-start | bytes 4194304 | tf_op jit(solution)/shard_map/all_to_all | solution.py:99
  33.3 0.5 broadcast.838
  33.7 0.6 reduce.6
  34.3 0.6 reduce.7
  36.1 0.5 copy.33
  37.2 0.7 fusion.89
  37.9 0.6 add_convert_fusion.3
  38.5 0.5 add_convert_fusion.2
  39.1 1.3 add_convert_fusion
  41.0 74.7 %all-to-all-done.1 = bf16[16,256,256]{2,1,0:T(8,128)(2,1)S(1)} async-done(((bf16[16,256,256]{2,1,0:T(8,128)(2,1)}), bf16[16,256,256]{2,1,0:T(8,128)(2,1)S(1)}, u32[]{:S(2)}, u32[]{:S(2)}) %all-to-all-start.1) | async-done | bytes 2097184 | tf_op jit(solution)/shard_map/all_to_all | solution.py:99
  115.7 1.5 gather_fusion.2
  117.2 1.3 broadcast_select_fusion.1
  118.5 54.8 %all-gather.2.cloned.1.call-done = f32[16,4,256,256]{3,2,1,0:T(8,128)} async-done(((f32[1,4,256,256]{3,2,1,0:T(8,128)}), f32[16,4,256,256]{3,2,1,0:T(8,128)}) %all-gather.2.cloned.1.call-update) | async-done | bytes 16777232 | tf_op jit(solution)/shard_map/all_gather | solution.py:103
  173.3 7.0 %reduce_sum.81 = bf16[4,256,256]{2,1,0:T(8,128)(2,1)S(1)} reduce(f32[16,4,256,256]{3,2,1,0:T(8,128)} %all-gather.2.cloned.1.call-done, f32[]{:T(128)} %constant.147.clone.1), dimensions={0}, to_apply=%region_1.2 | reduce | flops 3932160 | bytes 17301508 | tf_op jit(solution)/shard_map/reduce_sum | solution.py:102
  180.7 0.8 fusion.60
  181.5 1.3 fusion.93
  182.9 0.3 fusion.91
  183.3 0.3 fusion.56
  183.7 0.3 fusion.92
  184.0 0.5 copy-done
  184.9 0.3 fusion.90
  186.1 0.5 fusion.30
  186.6 0.5 fusion.28
  187.1 0.5 fusion.26
  187.6 0.4 fusion.24
  188.0 9.7 %while.14 = (s32[]{:T(128)}, f32[1024]{0:T(1024)S(1)}, f32[1024]{0:T(1024)S(1)}, f32[1024,128]{1,0:T(8,128)S(1)}, pred[3,2]{1,0:T(4,128)(4,1)S(1)}, /*index=5*/b...) while((s32[]{:T(128)}, f32[1024]{0:T(1024)S(1)}, ...), condition=%wide.region_16.17_spmd, body=%wide.region_13.16_spmd.sunk | while | flops 274902208 | bytes 13001355 | solution.py:145
  188.3 0.6 fusion.118
  188.9 0.5 bitcast_reduce_fusion.2
  189.4 0.6 fusion.122
  190.1 0.4 convert_reduce_fusion.7
  190.6 0.6 fusion.123
  191.5 0.6 fusion.118
  192.2 0.5 bitcast_reduce_fusion.2
  192.7 0.6 fusion.122
  193.3 0.4 convert_reduce_fusion.7
  193.8 0.6 fusion.123
  194.8 0.6 fusion.118
  195.4 0.5 bitcast_reduce_fusion.2
  195.9 0.6 fusion.122
  196.6 0.4 convert_reduce_fusion.7
  197.1 0.6 fusion.123
  197.9 0.8 convert_element_type.248
  (114 shorter events, 5.3 us)
Async XLA Ops:
  6.5 5.3 %copy-start.5 = (s32[1,6]{1,0:T(1,128)S(1)}, s32[1,6]{1,0:T(1,128)}, u32[]{:S(2)}) copy-start(s32[1,6]{1,0:T(1,128)} %param.17) | copy-start | bytes 76
  6.5 5.4 %copy-start.4 = (s32[1,6]{1,0:T(1,128)S(1)}, s32[1,6]{1,0:T(1,128)}, u32[]{:S(2)}) copy-start(s32[1,6]{1,0:T(1,128)} %param.19) | copy-start | bytes 76
  6.5 166.8 %all-gather.2.cloned.1.call-start = ((), (), s32[]{:S(2)}) async-start(), calls=%async_computation.2 | async-start | bytes 17825792 | tf_op jit(solution)/shard_map/all_gather | solution.py:103
  27.2 8.4 %copy-start.1 = (bf16[128,1024]{1,0:T(8,128)(2,1)S(1)}, bf16[128,1024]{1,0:T(8,128)(2,1)}, u32[]{:S(2)}) copy-start(bf16[128,1024]{1,0:T(8,128)(2,1)} %param.11) | copy-start | bytes 786436
  27.2 88.5 %all-to-all-start.1 = ((bf16[16,256,256]{2,1,0:T(8,128)(2,1)}), bf16[16,256,256]{2,1,0:T(8,128)(2,1)S(1)}, u32[]{:S(2)}, u32[]{:S(2)}) async-start(bf16[16,256,256]{2,1,0:T(8,128)(2,1)} %select_select_fusion), calls=%async_computation.1 | async-start | bytes 4194304 | tf_op jit(solution)/shard_map/all_to_all | solution.py:99
  35.5 1.4 slice-start
  35.7 1.5 copy-start.3
  183.3 1.2 copy-start
  184.9 0.8 copy-start.2
Sparse Core Ops, SparseCore 0:
  11.3 161.9 all-gather.1
